TPU v7x, 32 devices: a whole 2x2x4 slice. The times are simulated.
32 devices in a mesh: dom: 16 (over z, y, core), help: 2 (over x).
Axes of the slice: x: 2, y: 2, z: 4, core: 2. Of those that a mesh axis runs over, the one named last changes fastest.
Arguments:
- diag_blocks: float32 [256, 128, 128], P(('dom', 'help')), as said below
- up_blocks: float32 [256, 3, 128, 128], P(('dom', 'help')), as said below
- pattern: int32 [256, 6], P(('dom', 'help')), may hold values from 0 to 1, as said below
- vector_in: float32 [256, 128], P(('dom', 'help')), may hold values from -6 to 6
Outputs:
- factor: bfloat16 [256, 7, 128, 128], P(('dom', 'help'))
- applied: float32 [256, 128], P(('dom', 'help'))
Inputs may be any that keep to these rules, and one draw needn't show every extreme that they name: A one marks neighbour k of the block row (order +x, -x, +y, -y, +z, -z) as part of its FSAI pattern; ones only where that neighbour lies inside the grid; every block row has two or more ones. Of the 8 block rows of one device (an aligned run of 8 rows) at most 4 have more than two ones and the others have exactly two; the ones beyond the first two of each row number at most 16 on one device, and some device has exactly that many. Every diagonal block is symmetric; the matrix assembled from diag_blocks and up_blocks and every pattern's submatrix are positive definite. `up_blocks`: together with diag_blocks these blocks form the matrix described there.
All inputs are finite; a program needn't handle non-finite values.
Results may differ from a plain program's by a relative error of at most 0.011.
Values may be sent and summed in bfloat16 or wider, within the bound.
A program may use at most 64 MiB of HBM per device.

v0:
```python
import jax
import jax.numpy as jnp
from jax import lax
from jax.sharding import PartitionSpec as P

PLANE = 4


def passed_along(block, axis, distance):
    devices = range(lax.axis_size(axis))
    route = [(i - distance, i) for i in devices if i - distance in devices]
    return lax.ppermute(block, axis, route)


def edge_rows(payload_lower, payload_upper):
    received = []
    for shift_by, payload in ((1, payload_lower), (-1, payload_upper)):
        received.append(passed_along(payload, "help", shift_by))
    return received


def grid_faces(upward_y, downward, upward_z):
    received = []
    for shift_by, payload in ((1, upward_y), (-1, downward), (PLANE, upward_z), (-PLANE, downward)):
        received.append(passed_along(payload, "dom", shift_by))
    return received


def member_batch(far_blocks, coupling_blocks):
    solved = jax.scipy.linalg.cho_solve((far_blocks, True), jnp.swapaxes(coupling_blocks, -1, -2))
    contribution = jnp.einsum(
        "nab,nbc->nac", coupling_blocks, solved, precision=lax.Precision.HIGHEST
    )
    return (solved, contribution)


def build_rows(own_diag, near_diag, coupled, weights, member_limit, slot_total):
    row_total = own_diag.shape[0]
    block_width = own_diag.shape[1]
    highest = lax.Precision.HIGHEST
    identity = jnp.eye(block_width, dtype=jnp.float32)
    member_flags = weights > 0.5
    member_ranks = jnp.cumsum(member_flags.astype(jnp.int32), 1) - 1
    used = (member_flags & (member_ranks < member_limit)).reshape(row_total * 6)
    position = jnp.cumsum(used.astype(jnp.int32)) - 1
    target = jnp.where(used, position, 0)
    slot_ids = jnp.arange(slot_total, dtype=jnp.int32)
    matches = used[None, :] & (target[None, :] == slot_ids[:, None])
    source = jnp.sum(jnp.where(matches, jnp.arange(row_total * 6, dtype=jnp.int32)[None, :], 0), 1)
    alive = jnp.any(matches, 1)
    flat_diag = near_diag.reshape(row_total * 6, block_width, block_width)
    flat_coupled = coupled.reshape(row_total * 6, block_width, block_width)
    slot_far = jnp.where(alive[:, None, None], flat_diag[source], identity[None])
    slot_coupling = jnp.where(alive[:, None, None], flat_coupled[source], 0.0)
    solved, contribution = member_batch(slot_far, slot_coupling)
    solved_all = jnp.where(used[:, None, None], solved[target], 0.0).reshape(
        row_total, 6, block_width, block_width
    )
    schur_sum = jnp.sum(
        jnp.where(used[:, None, None], contribution[target], 0.0).reshape(
            row_total, 6, block_width, block_width
        ),
        1,
    )
    schur_block = own_diag - schur_sum
    inverse = jax.scipy.linalg.cho_solve(
        (jnp.linalg.cholesky(schur_block), True), jnp.broadcast_to(identity, schur_block.shape)
    )
    inverse = 0.5 * (inverse + jnp.swapaxes(inverse, -1, -2))
    upper_tri = jnp.swapaxes(jnp.linalg.cholesky(inverse), -1, -2)
    off_blocks = -jnp.einsum("rab,rkcb->rkac", upper_tri, solved_all, precision=highest)
    return jnp.concatenate([upper_tri[:, None], off_blocks], 1).astype(jnp.bfloat16)


def local(diag_blocks, up_blocks, pattern, vector_in):
    highest = lax.Precision.HIGHEST
    row_total = diag_blocks.shape[0]
    help_count = lax.axis_size("help")
    dom_count = lax.axis_size("dom")
    helper = lax.axis_index("help")
    domain = lax.axis_index("dom")
    coord_x = helper * row_total + jnp.arange(row_total, dtype=jnp.int32)
    line_length = row_total * help_count
    coord_y = domain % PLANE
    all_rows = (row_total,)
    validity = jnp.stack(
        [
            coord_x < line_length - 1,
            coord_x > 0,
            jnp.broadcast_to(coord_y < PLANE - 1, all_rows),
            jnp.broadcast_to(coord_y > 0, all_rows),
            jnp.broadcast_to(domain + PLANE < dom_count, all_rows),
            jnp.broadcast_to(domain >= PLANE, all_rows),
        ],
        1,
    )
    sent_diag = jnp.linalg.cholesky(diag_blocks)
    lower_x, upper_x = edge_rows(
        (sent_diag[-1:], up_blocks[-1:, 0], vector_in[-1:]), (sent_diag[:1], vector_in[:1])
    )
    lower_y, upper_y, lower_z, upper_z = grid_faces(
        (sent_diag, up_blocks[:, 1], vector_in),
        (sent_diag, vector_in),
        (sent_diag, up_blocks[:, 2], vector_in),
    )
    near_diag = jnp.stack(
        [
            jnp.concatenate([sent_diag[1:], upper_x[0]], 0),
            jnp.concatenate([lower_x[0], sent_diag[:-1]], 0),
            upper_y[0],
            lower_y[0],
            upper_z[0],
            lower_z[0],
        ],
        1,
    )
    coupled = jnp.stack(
        [
            up_blocks[:, 0],
            jnp.swapaxes(jnp.concatenate([lower_x[1], up_blocks[:-1, 0]], 0), -1, -2),
            up_blocks[:, 1],
            jnp.swapaxes(lower_y[1], -1, -2),
            up_blocks[:, 2],
            jnp.swapaxes(lower_z[1], -1, -2),
        ],
        1,
    )
    near_vec = jnp.stack(
        [
            jnp.concatenate([vector_in[1:], upper_x[1]], 0),
            jnp.concatenate([lower_x[2], vector_in[:-1]], 0),
            upper_y[1],
            lower_y[2],
            upper_z[1],
            lower_z[2],
        ],
        1,
    )
    far_terms = jnp.einsum("rkab,rkb->rka", coupled, near_vec, precision=highest)
    far_terms = jnp.where(validity[:, :, None], far_terms, 0.0)
    product = jnp.einsum("rab,rb->ra", diag_blocks, vector_in, precision=highest) + jnp.sum(
        far_terms, 1
    )
    weights = pattern.astype(jnp.float32)
    factor = build_rows(diag_blocks, near_diag, coupled, weights, 6, 4 * row_total)
    lower_xr, upper_xr = edge_rows((product[-1:],), (product[:1],))
    lower_yr, upper_yr, lower_zr, upper_zr = grid_faces((product,), (product,), (product,))
    near_prod = jnp.stack(
        [
            jnp.concatenate([product[1:], upper_xr[0]], 0),
            jnp.concatenate([lower_xr[0], product[:-1]], 0),
            upper_yr[0],
            lower_yr[0],
            upper_zr[0],
            lower_zr[0],
        ],
        1,
    )
    widened = factor.astype(jnp.float32)
    applied = jnp.einsum("rab,rb->ra", widened[:, 0], product, precision=highest)
    applied = applied + jnp.einsum("rkab,rkb->ra", widened[:, 1:], near_prod, precision=highest)
    return (factor, applied)


def solution(mesh):
    in_specs = (
        P(("dom", "help"), None, None),
        P(("dom", "help"), None, None, None),
        P(("dom", "help"), None),
        P(("dom", "help"), None),
    )
    out_specs = (P(("dom", "help"), None, None, None), P(("dom", "help"), None))
    return jax.shard_map(local, mesh=mesh, in_specs=in_specs, out_specs=out_specs, check_vma=False)
```

profile of v0, /device:TPU:0, one launch (start us, length us, event | category | flops | bytes accessed | tf_op | source)
XLA Modules:
  0.0 839.7 jit_solution(6082478202953883077)
XLA Ops:
  0.6 3.0 collective-permute-start.12
  4.9 7.8 collective-permute-start.14
  24.9 93.8 %custom-call.21 = f32[8,128,128]{2,1,0:T(8,128)S(1)} custom-call(f32[8,128,128]{2,1,0:T(8,128)S(1)} %fusion.32), custom_call_target="Cholesky" | custom-call | tf_op jit(solution)/shard_map/jit(cholesky)/cholesky | solution.py:97
  125.9 4.5 collective-permute-start.10
  135.9 8.4 collective-permute-start.8
  146.9 4.2 collective-permute-start
  159.8 4.5 collective-permute-start.4
  172.2 5.7 collective-permute-start.2
  185.6 3.9 copy.63
  189.5 3.9 gather_fusion.1
  193.4 3.2 fusion.6
  196.6 315.8 %custom-call.17 = f32[32,1,128,128]{2,3,1,0:T(8,128)} custom-call(f32[32,1,128,128]{3,2,1,0:T(8,128)} %fusion.6), custom_call_target="InvertDiagBlocksLowerTriangular" | custom-call | tf_op jit(solution)/shard_map/jit(_cho_solve)/vmap()/triangular_solve | solution.py:30
  515.7 5.0 fusion.44
  523.5 5.7 collective-permute-start.20
  530.6 2.6 gather_fusion
  534.9 5.3 fusion.4
  542.5 3.7 fusion.7
  546.2 2.4 gather_fusion.3
  554.7 94.0 %custom-call.22 = f32[8,128,128]{2,1,0:T(8,128)S(1)} custom-call(f32[8,128,128]{2,1,0:T(8,128)S(1)} %fusion.31), custom_call_target="Cholesky" | custom-call | tf_op jit(solution)/shard_map/jit(cholesky)/cholesky | solution.py:67
  649.0 78.6 %custom-call.18 = f32[8,1,128,128]{2,3,1,0:T(8,128)S(1)} custom-call(f32[8,1,128,128]{3,2,1,0:T(8,128)S(1)} %fusion.33), custom_call_target="InvertDiagBlocksLowerTriangular" | custom-call | tf_op jit(solution)/shard_map/jit(_cho_solve)/vmap()/triangular_solve | solution.py:66
  729.8 94.0 %custom-call.23 = f32[8,128,128]{2,1,0:T(8,128)S(1)} custom-call(f32[8,128,128]{2,1,0:T(8,128)S(1)} %fusion.25), custom_call_target="Cholesky" | custom-call | tf_op jit(solution)/shard_map/jit(cholesky)/cholesky | solution.py:70
  824.2 4.7 fusion.14
  829.5 2.6 copy.73
  832.1 4.7 collective-permute-start.16
  (145 shorter events, 76.2 us)
Async XLA Ops:
  0.6 135.3 %collective-permute-start.12 = (f32[8,128]{1,0:T(8,128)}, f32[8,128]{1,0:T(8,128)}, u32[]{:S(2)}, u32[]{:S(2)}) collective-permute-start(f32[8,128]{1,0:T(8,128)} %param.8), channel_id=1, source_target_pairs={{0,2},{2,4},{4,6},{6,8},{8,10},{10,12},{12,14},{14,16},{16,18},{18... | collective-permute-start | bytes 12296 | tf_op jit(solution)/shard_map/ppermute | solution.py:12
  3.6 130.3 %collective-permute-start.11 = (f32[8,128]{1,0:T(8,128)}, f32[8,128]{1,0:T(8,128)}, u32[]{:S(2)}, u32[]{:S(2)}) collective-permute-start(f32[8,128]{1,0:T(8,128)} %param.8), channel_id=1, source_target_pairs={{2,0},{4,2},{6,4},{8,6},{10,8},{12,10},{14,12},{16,14},{18,16},{20... | collective-permute-start | bytes 12296 | tf_op jit(solution)/shard_map/ppermute | solution.py:12
  4.9 142.0 %collective-permute-start.14 = (f32[8,128]{1,0:T(8,128)}, f32[8,128]{1,0:T(8,128)}, u32[]{:S(2)}, u32[]{:S(2)}) collective-permute-start(f32[8,128]{1,0:T(8,128)} %param.8), channel_id=1, source_target_pairs={{0,8},{2,10},{4,12},{6,14},{8,16},{10,18},{12,20},{14,22},{16,24},... | collective-permute-start | bytes 12296 | tf_op jit(solution)/shard_map/ppermute | solution.py:12
  12.7 132.3 %collective-permute-start.13 = (f32[8,128]{1,0:T(8,128)}, f32[8,128]{1,0:T(8,128)}, u32[]{:S(2)}, u32[]{:S(2)}) collective-permute-start(f32[8,128]{1,0:T(8,128)} %param.8), channel_id=1, source_target_pairs={{8,0},{10,2},{12,4},{14,6},{16,8},{18,10},{20,12},{22,14},{24,16},... | collective-permute-start | bytes 12296 | tf_op jit(solution)/shard_map/ppermute | solution.py:12
  15.3 110.6 %collective-permute-start.9 = (f32[1,128]{1,0:T(1,128)S(1)}, f32[1,128]{1,0:T(1,128)S(1)}, u32[]{:S(2)}, u32[]{:S(2)}) collective-permute-start(f32[1,128]{1,0:T(1,128)S(1)} %get-tuple-element.27), channel_id=1, source_target_pairs={{1,0},{3,2},{5,4},{7,6},{9,8},{11,10},{13,12},{15,14},{17,16},{19,... | collective-permute-start | bytes 1544 | tf_op jit(solution)/shard_map/ppermute | solution.py:12
  23.6 95.4 %copy-start.4 = (f32[8,128,128]{1,2,0:T(8,128)}, f32[8,128,128]{1,2,0:T(8,128)S(1)}, u32[]{:S(2)}) copy-start(f32[8,128,128]{1,2,0:T(8,128)S(1)} %copy.66) | copy-start | bytes 1572868
  23.6 97.6 %copy-start.6 = (f32[8,128]{1,0:T(8,128)S(1)}, f32[8,128]{1,0:T(8,128)}, u32[]{:S(2)}) copy-start(f32[8,128]{1,0:T(8,128)} %param.8) | copy-start | bytes 12292
  125.9 5.9 collective-permute-start.10
  131.8 48.1 %collective-permute-start.6 = (f32[8,128,128]{2,1,0:T(8,128)}, f32[8,128,128]{2,1,0:T(8,128)}, u32[]{:S(2)}, u32[]{:S(2)}) collective-permute-start(f32[8,128,128]{2,1,0:T(8,128)} %copy-done.5), channel_id=1, source_target_pairs={{0,2},{2,4},{4,6},{6,8},{8,10},{10,12},{12,14},{14,16},{16,18},{18... | collective-permute-start | bytes 1572872 | tf_op jit(solution)/shard_map/ppermute | solution.py:12
  133.9 38.3 %collective-permute-start.5 = (f32[8,128,128]{2,1,0:T(8,128)}, f32[8,128,128]{2,1,0:T(8,128)}, u32[]{:S(2)}, u32[]{:S(2)}) collective-permute-start(f32[8,128,128]{2,1,0:T(8,128)} %copy-done.5), channel_id=1, source_target_pairs={{2,0},{4,2},{6,4},{8,6},{10,8},{12,10},{14,12},{16,14},{18,16},{20... | collective-permute-start | bytes 1572872 | tf_op jit(solution)/shard_map/ppermute | solution.py:12
  135.9 47.8 %collective-permute-start.8 = (f32[8,128,128]{2,1,0:T(8,128)}, f32[8,128,128]{2,1,0:T(8,128)}, u32[]{:S(2)}, u32[]{:S(2)}) collective-permute-start(f32[8,128,128]{2,1,0:T(8,128)} %copy-done.5), channel_id=1, source_target_pairs={{0,8},{2,10},{4,12},{6,14},{8,16},{10,18},{12,20},{14,22},{16,24},... | collective-permute-start | bytes 1572872 | tf_op jit(solution)/shard_map/ppermute | solution.py:12
  145.0 36.8 %collective-permute-start.7 = (f32[8,128,128]{2,1,0:T(8,128)}, f32[8,128,128]{2,1,0:T(8,128)}, u32[]{:S(2)}, u32[]{:S(2)}) collective-permute-start(f32[8,128,128]{2,1,0:T(8,128)} %copy-done.5), channel_id=1, source_target_pairs={{8,0},{10,2},{12,4},{14,6},{16,8},{18,10},{20,12},{22,14},{24,16},... | collective-permute-start | bytes 1572872 | tf_op jit(solution)/shard_map/ppermute | solution.py:12
  146.9 6.1 collective-permute-start
  153.0 6.8 collective-permute-start.3
  159.8 6.4 collective-permute-start.4
  166.2 346.1 %collective-permute-start.1 = (f32[8,128,128]{1,2,0:T(8,128)}, f32[8,128,128]{1,2,0:T(8,128)}, u32[]{:S(2)}, u32[]{:S(2)}) collective-permute-start(f32[8,128,128]{1,2,0:T(8,128)} %bitcast.151), channel_id=1, source_target_pairs={{0,2},{2,4},{4,6},{6,8},{8,10},{10,12},{12,14},{14,16},{16,18},{18... | collective-permute-start | bytes 1572872 | tf_op jit(solution)/shard_map/ppermute | solution.py:12
  172.2 342.3 %collective-permute-start.2 = (f32[8,128,128]{1,2,0:T(8,128)}, f32[8,128,128]{1,2,0:T(8,128)}, u32[]{:S(2)}, u32[]{:S(2)}) collective-permute-start(f32[8,128,128]{1,2,0:T(8,128)} %bitcast.152), channel_id=1, source_target_pairs={{0,8},{2,10},{4,12},{6,14},{8,16},{10,18},{12,20},{14,22},{16,24},... | collective-permute-start | bytes 1572872 | tf_op jit(solution)/shard_map/ppermute | solution.py:12
  515.7 14.9 %copy-start.2 = (f32[8,6,128,128]{3,2,1,0:T(8,128)}, f32[8,6,128,128]{3,2,1,0:T(8,128)S(1)}, u32[]{:S(2)}) copy-start(f32[8,6,128,128]{3,2,1,0:T(8,128)S(1)} %bitcast_dynamic-update-slice_fusion) | copy-start | bytes 9437188
  520.8 317.3 %collective-permute-start.18 = (f32[8,128]{1,0:T(8,128)S(1)}, f32[8,128]{1,0:T(8,128)S(1)}, u32[]{:S(2)}, u32[]{:S(2)}) collective-permute-start(f32[8,128]{1,0:T(8,128)S(1)} %add.95), channel_id=1, source_target_pairs={{0,2},{2,4},{4,6},{6,8},{8,10},{10,12},{12,14},{14,16},{16,18},{18... | collective-permute-start | bytes 12296 | tf_op jit(solution)/shard_map/ppermute | solution.py:12
  522.2 315.8 %collective-permute-start.17 = (f32[8,128]{1,0:T(8,128)S(1)}, f32[8,128]{1,0:T(8,128)S(1)}, u32[]{:S(2)}, u32[]{:S(2)}) collective-permute-start(f32[8,128]{1,0:T(8,128)S(1)} %add.95), channel_id=1, source_target_pairs={{2,0},{4,2},{6,4},{8,6},{10,8},{12,10},{14,12},{16,14},{18,16},{20... | collective-permute-start | bytes 12296 | tf_op jit(solution)/shard_map/ppermute | solution.py:12
  523.5 314.6 %collective-permute-start.20 = (f32[8,128]{1,0:T(8,128)S(1)}, f32[8,128]{1,0:T(8,128)S(1)}, u32[]{:S(2)}, u32[]{:S(2)}) collective-permute-start(f32[8,128]{1,0:T(8,128)S(1)} %add.95), channel_id=1, source_target_pairs={{0,8},{2,10},{4,12},{6,14},{8,16},{10,18},{12,20},{14,22},{16,24},... | collective-permute-start | bytes 12296 | tf_op jit(solution)/shard_map/ppermute | solution.py:12
  529.3 308.8 %collective-permute-start.19 = (f32[8,128]{1,0:T(8,128)S(1)}, f32[8,128]{1,0:T(8,128)S(1)}, u32[]{:S(2)}, u32[]{:S(2)}) collective-permute-start(f32[8,128]{1,0:T(8,128)S(1)} %add.95), channel_id=1, source_target_pairs={{8,0},{10,2},{12,4},{14,6},{16,8},{18,10},{20,12},{22,14},{24,16},... | collective-permute-start | bytes 12296 | tf_op jit(solution)/shard_map/ppermute | solution.py:12
  533.2 298.9 %collective-permute-start.15 = (f32[1,128]{1,0:T(1,128)S(1)}, f32[1,128]{1,0:T(1,128)S(1)}, u32[]{:S(2)}, u32[]{:S(2)}) collective-permute-start(f32[1,128]{1,0:T(1,128)S(1)} %get-tuple-element.23), channel_id=1, source_target_pairs={{1,0},{3,2},{5,4},{7,6},{9,8},{11,10},{13,12},{15,14},{17,16},{19,... | collective-permute-start | bytes 1544 | tf_op jit(solution)/shard_map/ppermute | solution.py:12
  832.1 5.9 collective-permute-start.16
  (7 other events, 28.9 us)
where the time goes:
time: 848 us; the launch traced here: 840 us
  other arithmetic  692 us (82%)
  starting transfers between devices  66.1 us (8%)
  local copies, waits for them, and re-layouts  51 us (6%)
  matrix products  25.6 us (3%)
    another operation x2, other arithmetic, member_batch(): jax.scipy.linalg.cho_solve((far_blocks, True), jnp.swapaxes(coupling_bloc...  319 us
    another operation x4, other arithmetic, build_rows(): upper_tri = jnp.swapaxes(jnp.linalg.cholesky(inverse), -1, -2)  94.2 us
    another operation x3, other arithmetic, build_rows(): jnp.linalg.cholesky(schur_block)  94.2 us
    another operation x3, other arithmetic, local(): sent_diag = jnp.linalg.cholesky(diag_blocks)  93.9 us
    another operation x2, other arithmetic, build_rows(): jax.scipy.linalg.cho_solve((jnp.linalg.cholesky(schur_block), True), jnp....  78.7 us
    ppermute x21, starting transfers between devices, passed_along(): return lax.ppermute(block, axis, route)  66.1 us
    unnamed x38, local copies, waits for them, and re-layouts  21.1 us
  transfers between devices with their start and end apart: 21, of which 3 were waited for; matrix products, arithmetic and copies ran while one was open for 91% of the time, Pallas kernels for 0%

commit v1 on v0

v1 whole, which is shorter than its diff:
```python
import jax
import jax.numpy as jnp
from jax import lax
from jax.experimental import pallas as pl
from jax.experimental.pallas import tpu as pltpu
from jax.sharding import PartitionSpec as P

PLANE = 4
SUB = 32
HIGH = lax.Precision.HIGHEST
F32 = jnp.float32
BF16 = jnp.bfloat16


def mm(a, b, ca, cb):
    return lax.dot_general(
        a, b, (((ca,), (cb,)), ((), ())), precision=HIGH, preferred_element_type=F32
    )


def mm1(a, b, ca, cb):
    return lax.dot_general(
        a.astype(BF16), b.astype(BF16), (((ca,), (cb,)), ((), ())), preferred_element_type=F32
    )


def small_factors(tiles):
    lane = lax.broadcasted_iota(jnp.int32, (8, 128), 1)
    sub = lax.broadcasted_iota(jnp.int32, (8, 128), 0)
    within = lane % SUB
    base = lane - within
    for j in range(SUB - 1, -1, -1):
        top, at = j // 8, j % 8
        here = within == j
        cols = [jnp.take_along_axis(tiles[t], base + j, axis=1) for t in range(top + 1)]
        scale = lax.rsqrt(cols[top][at : at + 1, :])
        row = jnp.where(here[:1], 1.0, tiles[top][at : at + 1, :]) * scale
        final = jnp.where(within[:1] >= j, row, 0.0)
        for t in range(top + 1):
            new = jnp.where(here, 0.0, tiles[t]) - (cols[t] * scale) * row
            if t == top:
                new = jnp.where(sub < at, new, jnp.where(sub == at, final, tiles[t]))
            tiles[t] = new
    return tiles


def ul_factors(work):
    count, width = work.shape[0], work.shape[1]
    pack = width // SUB
    lane = lax.broadcasted_iota(jnp.int32, (SUB, width), 1)
    sub = lax.broadcasted_iota(jnp.int32, (SUB, width), 0)
    owner = lane // SUB
    for j in range(pack - 1, -1, -1):
        lo = SUB * j
        packed = []
        panels = []
        for g in range(count // pack):
            block = jnp.zeros((SUB, width), F32)
            panel = []
            for b in range(pack):
                rows = work[g * pack + b, lo : lo + SUB, :]
                shift = (SUB * (b - j)) % width
                moved = pltpu.roll(rows, shift, 1) if shift else rows
                block = jnp.where(owner == b, moved, block)
                panel.append(jnp.where(owner == j, (lane - lo == sub).astype(F32), rows))
            packed.append([block[8 * t : 8 * t + 8] for t in range(SUB // 8)])
            panels.append(jnp.concatenate(panel, 0))
        for g in range(count // pack):
            small = jnp.concatenate(small_factors(packed[g]), 0)
            spread = jnp.concatenate(
                [jnp.where(owner == b, small, 0.0) for b in range(pack)], 0
            )
            scaled = mm(spread, panels[g], 1, 0)
            for b in range(pack):
                at = g * pack + b
                v = scaled[SUB * b : SUB * b + SUB]
                work[at, lo : lo + SUB, :] = jnp.where(lane >= lo, v, 0.0)
                if lo:
                    change = mm(v, v, 0, 0)
                    full = lax.broadcasted_iota(jnp.int32, (lo, width), 1) // SUB
                    work[at, :lo, :] = jnp.where(full == j, 0.0, work[at, :lo, :]) - change[:lo]


def inverse_kernel(diag_ref, inv_ref, low_ref, work):
    work[...] = diag_ref[...]
    ul_factors(work)

    def body(r, carry):
        y = work[r]
        inv = mm(y, y, 0, 0)
        inv_ref[r] = inv
        low_ref[r] = inv.astype(BF16)
        return carry

    lax.fori_loop(0, work.shape[0], body, 0)


def rows_kernel(
    pattern_ref, diag_ref, up_ref, ux_ref, dx_ref, cy_ref, cz_ref, yu_ref, yl_ref, zu_ref,
    zl_ref, prod_ref, near_ref, factor_ref, applied_ref, work, solved
):
    count = work.shape[0]

    def gather(r, carry):
        schur = diag_ref[r]

        def term(k, inv, coupling, plus, mul):
            w = pattern_ref[r, k].astype(F32) * mul(inv, coupling, 1, 1 if plus else 0)
            solved[r, k] = w
            return mul(coupling, w, 1 if plus else 0, 0)

        schur = schur - term(0, dx_ref[r + 2], ux_ref[r + 1], True, mm)
        schur = schur - term(1, dx_ref[r], ux_ref[r], False, mm)
        schur = schur - term(2, yu_ref[r], up_ref[r, 1], True, mm1)
        schur = schur - term(3, yl_ref[r], cy_ref[r], False, mm1)
        schur = schur - term(4, zu_ref[r], up_ref[r, 2], True, mm1)
        schur = schur - term(5, zl_ref[r], cz_ref[r], False, mm1)
        work[r] = schur
        return carry

    lax.fori_loop(0, count, gather, 0)
    ul_factors(work)

    def finish(r, carry):
        y = work[r]
        low = y.astype(BF16)
        factor_ref[r, 0] = low
        total = mm(prod_ref[...][None][0], low.astype(F32), 1, 1)
        for k in range(6):
            block = (-(mm if k < 2 else mm1)(y, solved[r, k], 1, 1)).astype(BF16)
            factor_ref[r, 1 + k] = block
            total = total + mm(near_ref[k], block.astype(F32), 1, 1)
        keep = lax.broadcasted_iota(jnp.int32, total.shape, 0) == r
        applied_ref[...] = jnp.where(keep, total, applied_ref[...])
        return carry

    applied_ref[...] = jnp.zeros_like(applied_ref)
    lax.fori_loop(0, count, finish, 0)


def passed_along(block, axis, distance):
    devices = range(lax.axis_size(axis))
    route = [(i - distance, i) for i in devices if i - distance in devices]
    return lax.ppermute(block, axis, route)


VM = pl.BlockSpec(memory_space=pltpu.VMEM)
SM = pl.BlockSpec(memory_space=pltpu.SMEM)


def local(diag_blocks, up_blocks, pattern, vector_in):
    rows, width = diag_blocks.shape[0], diag_blocks.shape[1]
    helper = lax.axis_index("help")
    domain = lax.axis_index("dom")
    help_count = lax.axis_size("help")
    dom_count = lax.axis_size("dom")
    inv, low = pl.pallas_call(
        inverse_kernel,
        out_shape=(
            jax.ShapeDtypeStruct((rows, width, width), F32),
            jax.ShapeDtypeStruct((rows, width, width), BF16),
        ),
        in_specs=[VM],
        out_specs=(VM, VM),
        scratch_shapes=[pltpu.VMEM((rows, width, width), F32)],
        name="inverses",
    )(diag_blocks)
    up_x = up_blocks[:, 0]
    c_y = passed_along(up_blocks[:, 1].astype(BF16), "dom", 1)
    c_z = passed_along(up_blocks[:, 2].astype(BF16), "dom", PLANE)
    c_x = passed_along(up_x[-1:], "help", 1)
    own_t = jnp.einsum("rdab,ra->drb", up_blocks, vector_in, precision=HIGH)

    def near_rows(vec, lower_edge, upper_edge, vec_low, axis_low):
        return vec

    def spread(vec):
        up_edge = passed_along(vec[:1], "help", -1)
        low_edge = passed_along(vec[-1:], "help", 1)
        return jnp.stack(
            [
                jnp.concatenate([vec[1:], up_edge], 0),
                jnp.concatenate([low_edge, vec[:-1]], 0),
                passed_along(vec, "dom", -1),
                passed_along(vec, "dom", 1),
                passed_along(vec, "dom", -PLANE),
                passed_along(vec, "dom", PLANE),
            ]
        )

    x_up = jnp.concatenate([vector_in[1:], passed_along(vector_in[:1], "help", -1)], 0)
    y_up = passed_along(vector_in, "dom", -1)
    z_up = passed_along(vector_in, "dom", -PLANE)
    x_low = jnp.concatenate([passed_along(own_t[0, -1:], "help", 1), own_t[0, :-1]], 0)
    y_low = passed_along(own_t[1], "dom", 1)
    z_low = passed_along(own_t[2], "dom", PLANE)
    coord_y = domain % PLANE
    zero = jnp.zeros_like(vector_in)
    uppers = jnp.stack(
        [
            x_up,
            jnp.where(coord_y < PLANE - 1, y_up, zero),
            jnp.where(domain + PLANE < dom_count, z_up, zero),
        ],
        1,
    )
    product = (
        jnp.einsum("rab,rb->ra", diag_blocks, vector_in, precision=HIGH)
        + jnp.einsum("rdab,rdb->ra", up_blocks, uppers, precision=HIGH)
        + x_low
        + jnp.where(coord_y > 0, y_low, zero)
        + jnp.where(domain >= PLANE, z_low, zero)
    )
    near = spread(product)
    d_x = jnp.concatenate(
        [passed_along(inv[-1:], "help", 1), inv, passed_along(inv[:1], "help", -1)], 0
    )
    u_x = jnp.concatenate([c_x, up_x], 0)
    yu = passed_along(low, "dom", -1)
    yl = passed_along(low, "dom", 1)
    zu = passed_along(low, "dom", -PLANE)
    zl = passed_along(low, "dom", PLANE)
    factor, applied = pl.pallas_call(
        rows_kernel,
        out_shape=(
            jax.ShapeDtypeStruct((rows, 7, width, width), BF16),
            jax.ShapeDtypeStruct((rows, width), F32),
        ),
        in_specs=[SM] + [VM] * 12,
        out_specs=(VM, VM),
        scratch_shapes=[
            pltpu.VMEM((rows, width, width), F32),
            pltpu.VMEM((rows, 6, width, width), F32),
        ],
        name="rows",
        compiler_params=pltpu.CompilerParams(vmem_limit_bytes=40 << 20),
    )(pattern, diag_blocks, up_blocks, u_x, d_x, c_y, c_z, yu, yl, zu, zl, product, near)
    return (factor, applied)


def solution(mesh):
    in_specs = (
        P(("dom", "help"), None, None),
        P(("dom", "help"), None, None, None),
        P(("dom", "help"), None),
        P(("dom", "help"), None),
    )
    out_specs = (P(("dom", "help"), None, None, None), P(("dom", "help"), None))
    return jax.shard_map(local, mesh=mesh, in_specs=in_specs, out_specs=out_specs, check_vma=False)
```

time: 848 us -> 153 us (0.18)
  the two profiles are of different devices: /device:TPU:0 before, /device:TPU:10 now
where the time goes in v1:
time: 153 us; the launch traced here: 152 us
  Pallas kernels  62.9 us (41%)
  starting transfers between devices  52.2 us (34%)
  waiting for transfers between devices  23.3 us (15%)
  matrix products  5.1 us (3%)
  local copies, waits for them, and re-layouts  4.82 us (3%)
  other arithmetic  2.82 us (2%)
    ppermute x21, starting transfers between devices, passed_along(): return lax.ppermute(block, axis, route)  52.2 us
    pallas_call x1, Pallas kernels, local(): pl.pallas_call(rows_kernel, out_shape=(jax.ShapeDtypeStruct((rows, 7, wid...  44.2 us
    ppermute x21, waiting for transfers between devices, passed_along(): return lax.ppermute(block, axis, route)  23.3 us
    pallas_call x1, Pallas kernels, local(): pl.pallas_call(inverse_kernel, out_shape=(jax.ShapeDtypeStruct((rows, wid...  18.8 us
  transfers between devices with their start and end apart: 21, of which 7 were waited for; matrix products, arithmetic and copies ran while one was open for 8% of the time, Pallas kernels for 12%

profile of v1, /device:TPU:10, one launch (start us, length us, event | category | flops | bytes accessed | tf_op | source)
XLA Modules:
  0.0 152.2 jit_solution(10050614132975518280)
XLA Ops:
  0.6 2.9 %collective-permute-start.10 = (f32[8,128]{1,0:T(8,128)}, f32[8,128]{1,0:T(8,128)}, u32[]{:S(2)}, u32[]{:S(2)}) collective-permute-start(f32[8,128]{1,0:T(8,128)} %param.7), channel_id=1, source_target_pairs={{2,0},{4,2},{6,4},{8,6},{10,8},{12,10},{14,12},{16,14},{18,16},{20... | collective-permute-start | bytes 12296 | tf_op jit(solution)/shard_map/ppermute | solution.py:144
  3.5 1.9 %collective-permute-start.11 = (f32[8,128]{1,0:T(8,128)}, f32[8,128]{1,0:T(8,128)}, u32[]{:S(2)}, u32[]{:S(2)}) collective-permute-start(f32[8,128]{1,0:T(8,128)} %param.7), channel_id=1, source_target_pairs={{8,0},{10,2},{12,4},{14,6},{16,8},{18,10},{20,12},{22,14},{24,16},... | collective-permute-start | bytes 12296 | tf_op jit(solution)/shard_map/ppermute | solution.py:144
  6.7 3.0 %collective-permute-start.9 = (f32[1,128]{1,0:T(1,128)}, f32[1,128]{1,0:T(1,128)}, u32[]{:S(2)}, u32[]{:S(2)}) collective-permute-start(f32[1,128]{1,0:T(1,128)} %slice.62), channel_id=1, source_target_pairs={{1,0},{3,2},{5,4},{7,6},{9,8},{11,10},{13,12},{15,14},{17,16},{19,... | collective-permute-start | bytes 1544 | tf_op jit(solution)/shard_map/ppermute | solution.py:144
  9.7 2.4 %fusion.8 = f32[8,1,3,128]{3,1,2,0:T(1,128)S(1)} fusion(f32[8,128,1,1]{1,2,3,0:T(1,128)} %bitcast.64, f32[8,3,128,128]{3,2,1,0:T(8,128)} %up_ref.1), kind=kOutput, calls=%fused_computation.33 | convolution fusion | flops 4718592 | bytes 1589248 | tf_op jit(solution)/shard_map/rdab,ra->drb/dot_general | solution.py:172
  14.5 1.9 %collective-permute-start.13 = (f32[8,128]{1,0:T(8,128)}, f32[8,128]{1,0:T(8,128)}, u32[]{:S(2)}, u32[]{:S(2)}) collective-permute-start(f32[8,128]{1,0:T(8,128)} %get-tuple-element.10), channel_id=1, source_target_pairs={{0,2},{2,4},{4,6},{6,8},{8,10},{10,12},{12,14},{14,16},{16,18},{18... | collective-permute-start | bytes 12296 | tf_op jit(solution)/shard_map/ppermute | solution.py:144
  17.3 18.8 %inverses.1 = (f32[8,128,128]{2,1,0:T(8,128)}, bf16[8,128,128]{2,1,0:T(8,128)(2,1)}) custom-call(f32[8,128,128]{2,1,0:T(8,128)} %diag_ref.3), custom_call_target="tpu_custom_call" | custom-call | tf_op jit(solution)/shard_map/inverses/pallas_call | solution.py:157
  38.6 4.0 %collective-permute-start.14 = (f32[8,128]{1,0:T(8,128)}, f32[8,128]{1,0:T(8,128)S(1)}, u32[]{:S(2)}, u32[]{:S(2)}) collective-permute-start(f32[8,128]{1,0:T(8,128)} %get-tuple-element.11), channel_id=1, source_target_pairs={{0,8},{2,10},{4,12},{6,14},{8,16},{10,18},{12,20},{14,22},{16,24},... | collective-permute-start | bytes 12296 | tf_op jit(solution)/shard_map/ppermute | solution.py:144
  45.4 4.0 %collective-permute-start.4 = (bf16[8,128,128]{2,1,0:T(8,128)(2,1)}, bf16[8,128,128]{2,1,0:T(8,128)(2,1)S(1)}, u32[]{:S(2)}, u32[]{:S(2)}) collective-permute-start(bf16[8,128,128]{2,1,0:T(8,128)(2,1)} %get-tuple-element.6), channel_id=1, source_target_pairs={{0,8},{2,10},{4,12},{6,14},{8,16},{10,18},{12,20},{14,22},{16,24},... | collective-permute-start | bytes 786440 | tf_op jit(solution)/shard_map/ppermute | solution.py:144
  53.2 5.1 %collective-permute-start.2 = (f32[1,128,128]{2,1,0:T(8,128)S(1)}, f32[1,128,128]{2,1,0:T(8,128)S(1)}, u32[]{:S(2)}, u32[]{:S(2)}) collective-permute-start(f32[1,128,128]{2,1,0:T(8,128)S(1)} %get-tuple-element.9), channel_id=1, source_target_pairs={{1,0},{3,2},{5,4},{7,6},{9,8},{11,10},{13,12},{15,14},{17,16},{19,... | collective-permute-start | bytes 196616 | tf_op jit(solution)/shard_map/ppermute | solution.py:144
  62.9 4.1 %collective-permute-done.16 = f32[1,128]{1,0:T(1,128)S(1)} collective-permute-done((f32[1,128]{1,0:T(1,128)S(1)}, f32[1,128]{1,0:T(1,128)S(1)}, u32[]{:S(2)}, u32[]{:S(2)}) %collective-permute-start.16) | collective-permute-done | bytes 544 | tf_op jit(solution)/shard_map/ppermute | solution.py:144
  67.0 1.9 %collective-permute-start.17 = (f32[8,128]{1,0:T(8,128)S(1)}, f32[8,128]{1,0:T(8,128)S(1)}, u32[]{:S(2)}, u32[]{:S(2)}) collective-permute-start(f32[8,128]{1,0:T(8,128)S(1)} %fusion.3.prod_ref), channel_id=1, source_target_pairs={{2,0},{4,2},{6,4},{8,6},{10,8},{12,10},{14,12},{16,14},{18,16},{20... | collective-permute-start | bytes 12296 | tf_op jit(solution)/shard_map/ppermute | solution.py:144
  70.2 2.7 %collective-permute-start.18 = (f32[8,128]{1,0:T(8,128)S(1)}, f32[8,128]{1,0:T(8,128)S(1)}, u32[]{:S(2)}, u32[]{:S(2)}) collective-permute-start(f32[8,128]{1,0:T(8,128)S(1)} %fusion.3.prod_ref), channel_id=1, source_target_pairs={{0,2},{2,4},{4,6},{6,8},{8,10},{10,12},{12,14},{14,16},{16,18},{18... | collective-permute-start | bytes 12296 | tf_op jit(solution)/shard_map/ppermute | solution.py:144
  73.0 3.1 %collective-permute-done.18 = f32[8,128]{1,0:T(8,128)S(1)} collective-permute-done((f32[8,128]{1,0:T(8,128)S(1)}, f32[8,128]{1,0:T(8,128)S(1)}, u32[]{:S(2)}, u32[]{:S(2)}) %collective-permute-start.18) | collective-permute-done | bytes 4128 | tf_op jit(solution)/shard_map/ppermute | solution.py:144
  76.1 1.9 %collective-permute-start.19 = (f32[8,128]{1,0:T(8,128)S(1)}, f32[8,128]{1,0:T(8,128)S(1)}, u32[]{:S(2)}, u32[]{:S(2)}) collective-permute-start(f32[8,128]{1,0:T(8,128)S(1)} %fusion.3.prod_ref), channel_id=1, source_target_pairs={{8,0},{10,2},{12,4},{14,6},{16,8},{18,10},{20,12},{22,14},{24,16},... | collective-permute-start | bytes 12296 | tf_op jit(solution)/shard_map/ppermute | solution.py:144
  78.0 3.6 %collective-permute-done.19 = f32[8,128]{1,0:T(8,128)S(1)} collective-permute-done((f32[8,128]{1,0:T(8,128)S(1)}, f32[8,128]{1,0:T(8,128)S(1)}, u32[]{:S(2)}, u32[]{:S(2)}) %collective-permute-start.19) | collective-permute-done | bytes 4128 | tf_op jit(solution)/shard_map/ppermute | solution.py:144
  81.5 1.9 %collective-permute-start.20 = (f32[8,128]{1,0:T(8,128)S(1)}, f32[8,128]{1,0:T(8,128)S(1)}, u32[]{:S(2)}, u32[]{:S(2)}) collective-permute-start(f32[8,128]{1,0:T(8,128)S(1)} %fusion.3.prod_ref), channel_id=1, source_target_pairs={{0,8},{2,10},{4,12},{6,14},{8,16},{10,18},{12,20},{14,22},{16,24},... | collective-permute-start | bytes 12296 | tf_op jit(solution)/shard_map/ppermute | solution.py:144
  83.5 3.6 %collective-permute-done.20 = f32[8,128]{1,0:T(8,128)S(1)} collective-permute-done((f32[8,128]{1,0:T(8,128)S(1)}, f32[8,128]{1,0:T(8,128)S(1)}, u32[]{:S(2)}, u32[]{:S(2)}) %collective-permute-start.20) | collective-permute-done | bytes 4128 | tf_op jit(solution)/shard_map/ppermute | solution.py:144
  87.0 1.9 %collective-permute-start.8 = (bf16[8,128,128]{2,1,0:T(8,128)(2,1)S(1)}, bf16[8,128,128]{2,1,0:T(8,128)(2,1)S(1)}, u32[]{:S(2)}, u32[]{:S(2)}) collective-permute-start(bf16[8,128,128]{2,1,0:T(8,128)(2,1)S(1)} %copy-done.6), channel_id=1, source_target_pairs={{0,8},{2,10},{4,12},{6,14},{8,16},{10,18},{12,20},{14,22},{16,24},... | collective-permute-start | bytes 786440 | tf_op jit(solution)/shard_map/ppermute | solution.py:144
  89.0 3.9 %collective-permute-start.7 = (bf16[8,128,128]{2,1,0:T(8,128)(2,1)S(1)}, bf16[8,128,128]{2,1,0:T(8,128)(2,1)S(1)}, u32[]{:S(2)}, u32[]{:S(2)}) collective-permute-start(bf16[8,128,128]{2,1,0:T(8,128)(2,1)S(1)} %copy-done.6), channel_id=1, source_target_pairs={{8,0},{10,2},{12,4},{14,6},{16,8},{18,10},{20,12},{22,14},{24,16},... | collective-permute-start | bytes 786440 | tf_op jit(solution)/shard_map/ppermute | solution.py:144
  92.9 1.9 %collective-permute-start.6 = (bf16[8,128,128]{2,1,0:T(8,128)(2,1)S(1)}, bf16[8,128,128]{2,1,0:T(8,128)(2,1)S(1)}, u32[]{:S(2)}, u32[]{:S(2)}) collective-permute-start(bf16[8,128,128]{2,1,0:T(8,128)(2,1)S(1)} %copy-done.6), channel_id=1, source_target_pairs={{0,2},{2,4},{4,6},{6,8},{8,10},{10,12},{12,14},{14,16},{16,18},{18... | collective-permute-start | bytes 786440 | tf_op jit(solution)/shard_map/ppermute | solution.py:144
  94.9 4.5 %collective-permute-start.5 = (bf16[8,128,128]{2,1,0:T(8,128)(2,1)S(1)}, bf16[8,128,128]{2,1,0:T(8,128)(2,1)S(1)}, u32[]{:S(2)}, u32[]{:S(2)}) collective-permute-start(bf16[8,128,128]{2,1,0:T(8,128)(2,1)S(1)} %copy-done.6), channel_id=1, source_target_pairs={{2,0},{4,2},{6,4},{8,6},{10,8},{12,10},{14,12},{16,14},{18,16},{20... | collective-permute-start | bytes 786440 | tf_op jit(solution)/shard_map/ppermute | solution.py:144
  99.4 2.1 %collective-permute-start.3 = (bf16[8,128,128]{2,1,0:T(8,128)(2,1)S(1)}, bf16[8,128,128]{2,1,0:T(8,128)(2,1)S(1)}, u32[]{:S(2)}, u32[]{:S(2)}) collective-permute-start(bf16[8,128,128]{2,1,0:T(8,128)(2,1)S(1)} %get-tuple-element.7), channel_id=1, source_target_pairs={{0,2},{2,4},{4,6},{6,8},{8,10},{10,12},{12,14},{14,16},{16,18},{18... | collective-permute-start | bytes 786440 | tf_op jit(solution)/shard_map/ppermute | solution.py:144
  101.6 6.4 %collective-permute-done.3.cy_ref = bf16[8,128,128]{2,1,0:T(8,128)(2,1)S(1)} collective-permute-done((bf16[8,128,128]{2,1,0:T(8,128)(2,1)S(1)}, bf16[8,128,128]{2,1,0:T(8,128)(2,1)S(1)}, u32[]{:S(2)}, u32[]{:S(2)}) %collective-permute-start.3) | collective-permute-done | bytes 262176 | tf_op jit(solution)/shard_map/ppermute | solution.py:144
  108.0 44.2 %rows.1 = (bf16[8,7,128,128]{3,2,1,0:T(8,128)(2,1)}, f32[8,128]{1,0:T(8,128)}) custom-call(s32[8,6]{1,0:T(8,128)S(1)} %copy-done.2, f32[8,128,128]{2,1,0:T(8,128)S(1)} %copy-done.1, f32[8,3,128,128]{3,2,1,0:T(8,128)S(1)} %copy-done, f32[9,128,128]{2,1,0:T(8,128)S(1)} %pad_maximum_fusion.1.ux_ref, f32[10,128,128]{2,1,0:T(8,128)S(1)} %pad_maximum_fusion.dx_ref, ...), custom_call_target="tpu_custom_call" | custom-call | tf_op jit(solution)/shard_map/rows/pallas_call | solution.py:223
  (62 shorter events, 19.4 us)
Async XLA Ops:
  0.6 42.7 %collective-permute-start.10 = (f32[8,128]{1,0:T(8,128)}, f32[8,128]{1,0:T(8,128)}, u32[]{:S(2)}, u32[]{:S(2)}) collective-permute-start(f32[8,128]{1,0:T(8,128)} %param.7), channel_id=1, source_target_pairs={{2,0},{4,2},{6,4},{8,6},{10,8},{12,10},{14,12},{16,14},{18,16},{20... | collective-permute-start | bytes 12296 | tf_op jit(solution)/shard_map/ppermute | solution.py:144
  3.5 41.8 %collective-permute-start.11 = (f32[8,128]{1,0:T(8,128)}, f32[8,128]{1,0:T(8,128)}, u32[]{:S(2)}, u32[]{:S(2)}) collective-permute-start(f32[8,128]{1,0:T(8,128)} %param.7), channel_id=1, source_target_pairs={{8,0},{10,2},{12,4},{14,6},{16,8},{18,10},{20,12},{22,14},{24,16},... | collective-permute-start | bytes 12296 | tf_op jit(solution)/shard_map/ppermute | solution.py:144
  6.7 32.0 %collective-permute-start.9 = (f32[1,128]{1,0:T(1,128)}, f32[1,128]{1,0:T(1,128)}, u32[]{:S(2)}, u32[]{:S(2)}) collective-permute-start(f32[1,128]{1,0:T(1,128)} %slice.62), channel_id=1, source_target_pairs={{1,0},{3,2},{5,4},{7,6},{9,8},{11,10},{13,12},{15,14},{17,16},{19,... | collective-permute-start | bytes 1544 | tf_op jit(solution)/shard_map/ppermute | solution.py:144
  12.7 39.3 %collective-permute-start.12 = (f32[1,128]{1,0:T(1,128)}, f32[1,128]{1,0:T(1,128)}, u32[]{:S(2)}, u32[]{:S(2)}) collective-permute-start(f32[1,128]{1,0:T(1,128)} %slice_bitcast_fusion.7), channel_id=1, source_target_pairs={{0,1},{2,3},{4,5},{6,7},{8,9},{10,11},{12,13},{14,15},{16,17},{18,... | collective-permute-start | bytes 1544 | tf_op jit(solution)/shard_map/ppermute | solution.py:144
  14.5 38.7 %collective-permute-start.13 = (f32[8,128]{1,0:T(8,128)}, f32[8,128]{1,0:T(8,128)}, u32[]{:S(2)}, u32[]{:S(2)}) collective-permute-start(f32[8,128]{1,0:T(8,128)} %get-tuple-element.10), channel_id=1, source_target_pairs={{0,2},{2,4},{4,6},{6,8},{8,10},{10,12},{12,14},{14,16},{16,18},{18... | collective-permute-start | bytes 12296 | tf_op jit(solution)/shard_map/ppermute | solution.py:144
  37.0 64.6 %copy-start.3 = (f32[8,128,128]{2,1,0:T(8,128)S(1)}, f32[8,128,128]{2,1,0:T(8,128)}, u32[]{:S(2)}) copy-start(f32[8,128,128]{2,1,0:T(8,128)} %get-tuple-element.4) | copy-start | bytes 1572868
  38.6 48.4 %copy-start.6 = (bf16[8,128,128]{2,1,0:T(8,128)(2,1)S(1)}, bf16[8,128,128]{2,1,0:T(8,128)(2,1)}, u32[]{:S(2)}) copy-start(bf16[8,128,128]{2,1,0:T(8,128)(2,1)} %get-tuple-element.5) | copy-start | bytes 786436
  38.6 19.7 %collective-permute-start.14 = (f32[8,128]{1,0:T(8,128)}, f32[8,128]{1,0:T(8,128)S(1)}, u32[]{:S(2)}, u32[]{:S(2)}) collective-permute-start(f32[8,128]{1,0:T(8,128)} %get-tuple-element.11), channel_id=1, source_target_pairs={{0,8},{2,10},{4,12},{6,14},{8,16},{10,18},{12,20},{14,22},{16,24},... | collective-permute-start | bytes 12296 | tf_op jit(solution)/shard_map/ppermute | solution.py:144
  43.4 45.6 %collective-permute-start = (f32[1,128,128]{2,1,0:T(8,128)S(1)}, f32[1,128,128]{2,1,0:T(8,128)S(1)}, u32[]{:S(2)}, u32[]{:S(2)}) collective-permute-start(f32[1,128,128]{2,1,0:T(8,128)S(1)} %slice_bitcast_fusion.3), channel_id=1, source_target_pairs={{0,1},{2,3},{4,5},{6,7},{8,9},{10,11},{12,13},{14,15},{16,17},{18,... | collective-permute-start | bytes 196616 | tf_op jit(solution)/shard_map/ppermute | solution.py:144
  45.4 54.0 %collective-permute-start.4 = (bf16[8,128,128]{2,1,0:T(8,128)(2,1)}, bf16[8,128,128]{2,1,0:T(8,128)(2,1)S(1)}, u32[]{:S(2)}, u32[]{:S(2)}) collective-permute-start(bf16[8,128,128]{2,1,0:T(8,128)(2,1)} %get-tuple-element.6), channel_id=1, source_target_pairs={{0,8},{2,10},{4,12},{6,14},{8,16},{10,18},{12,20},{14,22},{16,24},... | collective-permute-start | bytes 786440 | tf_op jit(solution)/shard_map/ppermute | solution.py:144
  51.9 56.1 %copy-start.2 = (s32[8,6]{1,0:T(8,128)S(1)}, s32[8,6]{1,0:T(8,128)}, u32[]{:S(2)}) copy-start(s32[8,6]{1,0:T(8,128)} %pattern_ref.1) | copy-start | bytes 580
  51.9 41.0 %collective-permute-start.1 = (f32[1,128,128]{2,1,0:T(8,128)S(1)}, f32[1,128,128]{2,1,0:T(8,128)S(1)}, u32[]{:S(2)}, u32[]{:S(2)}) collective-permute-start(f32[1,128,128]{2,1,0:T(8,128)S(1)} %copy-done.4), channel_id=1, source_target_pairs={{0,1},{2,3},{4,5},{6,7},{8,9},{10,11},{12,13},{14,15},{16,17},{18,... | collective-permute-start | bytes 196616 | tf_op jit(solution)/shard_map/ppermute | solution.py:144
  53.2 41.6 %collective-permute-start.2 = (f32[1,128,128]{2,1,0:T(8,128)S(1)}, f32[1,128,128]{2,1,0:T(8,128)S(1)}, u32[]{:S(2)}, u32[]{:S(2)}) collective-permute-start(f32[1,128,128]{2,1,0:T(8,128)S(1)} %get-tuple-element.9), channel_id=1, source_target_pairs={{1,0},{3,2},{5,4},{7,6},{9,8},{11,10},{13,12},{15,14},{17,16},{19,... | collective-permute-start | bytes 196616 | tf_op jit(solution)/shard_map/ppermute | solution.py:144
  59.0 2.6 %collective-permute-start.15 = (f32[1,128]{1,0:T(1,128)S(1)}, f32[1,128]{1,0:T(1,128)S(1)}, u32[]{:S(2)}, u32[]{:S(2)}) collective-permute-start(f32[1,128]{1,0:T(1,128)S(1)} %get-tuple-element.13), channel_id=1, source_target_pairs={{1,0},{3,2},{5,4},{7,6},{9,8},{11,10},{13,12},{15,14},{17,16},{19,... | collective-permute-start | bytes 1544 | tf_op jit(solution)/shard_map/ppermute | solution.py:144
  61.6 5.5 %collective-permute-start.16 = (f32[1,128]{1,0:T(1,128)S(1)}, f32[1,128]{1,0:T(1,128)S(1)}, u32[]{:S(2)}, u32[]{:S(2)}) collective-permute-start(f32[1,128]{1,0:T(1,128)S(1)} %get-tuple-element.12), channel_id=1, source_target_pairs={{0,1},{2,3},{4,5},{6,7},{8,9},{10,11},{12,13},{14,15},{16,17},{18,... | collective-permute-start | bytes 1544 | tf_op jit(solution)/shard_map/ppermute | solution.py:144
  67.0 3.2 %collective-permute-start.17 = (f32[8,128]{1,0:T(8,128)S(1)}, f32[8,128]{1,0:T(8,128)S(1)}, u32[]{:S(2)}, u32[]{:S(2)}) collective-permute-start(f32[8,128]{1,0:T(8,128)S(1)} %fusion.3.prod_ref), channel_id=1, source_target_pairs={{2,0},{4,2},{6,4},{8,6},{10,8},{12,10},{14,12},{16,14},{18,16},{20... | collective-permute-start | bytes 12296 | tf_op jit(solution)/shard_map/ppermute | solution.py:144
  70.2 5.8 %collective-permute-start.18 = (f32[8,128]{1,0:T(8,128)S(1)}, f32[8,128]{1,0:T(8,128)S(1)}, u32[]{:S(2)}, u32[]{:S(2)}) collective-permute-start(f32[8,128]{1,0:T(8,128)S(1)} %fusion.3.prod_ref), channel_id=1, source_target_pairs={{0,2},{2,4},{4,6},{6,8},{8,10},{10,12},{12,14},{14,16},{16,18},{18... | collective-permute-start | bytes 12296 | tf_op jit(solution)/shard_map/ppermute | solution.py:144
  76.1 5.5 %collective-permute-start.19 = (f32[8,128]{1,0:T(8,128)S(1)}, f32[8,128]{1,0:T(8,128)S(1)}, u32[]{:S(2)}, u32[]{:S(2)}) collective-permute-start(f32[8,128]{1,0:T(8,128)S(1)} %fusion.3.prod_ref), channel_id=1, source_target_pairs={{8,0},{10,2},{12,4},{14,6},{16,8},{18,10},{20,12},{22,14},{24,16},... | collective-permute-start | bytes 12296 | tf_op jit(solution)/shard_map/ppermute | solution.py:144
  81.5 5.5 %collective-permute-start.20 = (f32[8,128]{1,0:T(8,128)S(1)}, f32[8,128]{1,0:T(8,128)S(1)}, u32[]{:S(2)}, u32[]{:S(2)}) collective-permute-start(f32[8,128]{1,0:T(8,128)S(1)} %fusion.3.prod_ref), channel_id=1, source_target_pairs={{0,8},{2,10},{4,12},{6,14},{8,16},{10,18},{12,20},{14,22},{16,24},... | collective-permute-start | bytes 12296 | tf_op jit(solution)/shard_map/ppermute | solution.py:144
  87.0 21.0 %collective-permute-start.8 = (bf16[8,128,128]{2,1,0:T(8,128)(2,1)S(1)}, bf16[8,128,128]{2,1,0:T(8,128)(2,1)S(1)}, u32[]{:S(2)}, u32[]{:S(2)}) collective-permute-start(bf16[8,128,128]{2,1,0:T(8,128)(2,1)S(1)} %copy-done.6), channel_id=1, source_target_pairs={{0,8},{2,10},{4,12},{6,14},{8,16},{10,18},{12,20},{14,22},{16,24},... | collective-permute-start | bytes 786440 | tf_op jit(solution)/shard_map/ppermute | solution.py:144
  89.0 19.0 %collective-permute-start.7 = (bf16[8,128,128]{2,1,0:T(8,128)(2,1)S(1)}, bf16[8,128,128]{2,1,0:T(8,128)(2,1)S(1)}, u32[]{:S(2)}, u32[]{:S(2)}) collective-permute-start(bf16[8,128,128]{2,1,0:T(8,128)(2,1)S(1)} %copy-done.6), channel_id=1, source_target_pairs={{8,0},{10,2},{12,4},{14,6},{16,8},{18,10},{20,12},{22,14},{24,16},... | collective-permute-start | bytes 786440 | tf_op jit(solution)/shard_map/ppermute | solution.py:144
  92.9 15.1 %collective-permute-start.6 = (bf16[8,128,128]{2,1,0:T(8,128)(2,1)S(1)}, bf16[8,128,128]{2,1,0:T(8,128)(2,1)S(1)}, u32[]{:S(2)}, u32[]{:S(2)}) collective-permute-start(bf16[8,128,128]{2,1,0:T(8,128)(2,1)S(1)} %copy-done.6), channel_id=1, source_target_pairs={{0,2},{2,4},{4,6},{6,8},{8,10},{10,12},{12,14},{14,16},{16,18},{18... | collective-permute-start | bytes 786440 | tf_op jit(solution)/shard_map/ppermute | solution.py:144
  94.9 13.2 %collective-permute-start.5 = (bf16[8,128,128]{2,1,0:T(8,128)(2,1)S(1)}, bf16[8,128,128]{2,1,0:T(8,128)(2,1)S(1)}, u32[]{:S(2)}, u32[]{:S(2)}) collective-permute-start(bf16[8,128,128]{2,1,0:T(8,128)(2,1)S(1)} %copy-done.6), channel_id=1, source_target_pairs={{2,0},{4,2},{6,4},{8,6},{10,8},{12,10},{14,12},{16,14},{18,16},{20... | collective-permute-start | bytes 786440 | tf_op jit(solution)/shard_map/ppermute | solution.py:144
  99.4 8.6 %collective-permute-start.3 = (bf16[8,128,128]{2,1,0:T(8,128)(2,1)S(1)}, bf16[8,128,128]{2,1,0:T(8,128)(2,1)S(1)}, u32[]{:S(2)}, u32[]{:S(2)}) collective-permute-start(bf16[8,128,128]{2,1,0:T(8,128)(2,1)S(1)} %get-tuple-element.7), channel_id=1, source_target_pairs={{0,2},{2,4},{4,6},{6,8},{8,10},{10,12},{12,14},{14,16},{16,18},{18... | collective-permute-start | bytes 786440 | tf_op jit(solution)/shard_map/ppermute | solution.py:144
  (4 other events, 77.2 us)

commit v2 on v1

v2 whole, which is shorter than its diff:
```python
import functools

import jax
import jax.numpy as jnp
from jax import lax
from jax.experimental import pallas as pl
from jax.experimental.pallas import tpu as pltpu
from jax.sharding import PartitionSpec as P

PLANE = 4
SUB = 32
MESSAGES = 25
HIGH = lax.Precision.HIGHEST
F32 = jnp.float32
BF16 = jnp.bfloat16


def mm(a, b, ca, cb):
    return lax.dot_general(
        a, b, (((ca,), (cb,)), ((), ())), precision=HIGH, preferred_element_type=F32
    )


def mm1(a, b, ca, cb):
    return lax.dot_general(
        a.astype(BF16), b.astype(BF16), (((ca,), (cb,)), ((), ())), preferred_element_type=F32
    )


def halves(a):
    high = a.astype(BF16)
    return high, (a - high.astype(F32)).astype(BF16)


def mm3(a, b, ca, cb):
    (ah, al), (bh, bl) = halves(a), halves(b)
    return mm1(ah, bh, ca, cb) + (mm1(ah, bl, ca, cb) + mm1(al, bh, ca, cb))


def small_factors(tiles):
    lane = lax.broadcasted_iota(jnp.int32, (8, 128), 1)
    sub = lax.broadcasted_iota(jnp.int32, (8, 128), 0)
    within = lane % SUB
    base = lane - within
    for j in range(SUB - 1, -1, -1):
        top, at = j // 8, j % 8
        here = within == j
        cols = [jnp.take_along_axis(tiles[t], base + j, axis=1) for t in range(top + 1)]
        scale = lax.rsqrt(cols[top][at : at + 1, :])
        row = jnp.where(here[:1], 1.0, tiles[top][at : at + 1, :]) * scale
        final = jnp.where(within[:1] >= j, row, 0.0)
        for t in range(top + 1):
            new = jnp.where(here, 0.0, tiles[t]) - (cols[t] * scale) * row
            if t == top:
                new = jnp.where(sub < at, new, jnp.where(sub == at, final, tiles[t]))
            tiles[t] = new
    return tiles


def ul_factors(work, between=None):
    count, width = work.shape[0], work.shape[1]
    pack = width // SUB
    lane = lax.broadcasted_iota(jnp.int32, (SUB, width), 1)
    sub = lax.broadcasted_iota(jnp.int32, (SUB, width), 0)
    owner = lane // SUB
    for j in range(pack - 1, -1, -1):
        lo = SUB * j
        packed = []
        panels = []
        for g in range(count // pack):
            block = jnp.zeros((SUB, width), F32)
            panel = []
            for b in range(pack):
                rows = work[g * pack + b, lo : lo + SUB, :]
                shift = (SUB * (b - j)) % width
                moved = pltpu.roll(rows, shift, 1) if shift else rows
                block = jnp.where(owner == b, moved, block)
                panel.append(jnp.where(owner == j, (lane - lo == sub).astype(F32), rows))
            packed.append([block[8 * t : 8 * t + 8] for t in range(SUB // 8)])
            panels.append(jnp.concatenate(panel, 0))
        for g in range(count // pack):
            small = jnp.concatenate(small_factors(packed[g]), 0)
            spread = jnp.concatenate(
                [jnp.where(owner == b, small, 0.0) for b in range(pack)], 0
            )
            scaled = mm(spread, panels[g], 1, 0)
            for b in range(pack):
                at = g * pack + b
                v = scaled[SUB * b : SUB * b + SUB]
                work[at, lo : lo + SUB, :] = jnp.where(lane >= lo, v, 0.0)
                if lo:
                    change = mm(v, v, 0, 0)
                    full = lax.broadcasted_iota(jnp.int32, (lo, width), 1) // SUB
                    work[at, :lo, :] = jnp.where(full == j, 0.0, work[at, :lo, :]) - change[:lo]
        if between:
            between(j)


def exchange_kernel(
    line_count, dom_count, diag_ref, up_ref, x_ref, prod_ref, near_ref, dx_ref, edge_ref, cy_ref,
    cz_ref, yu_ref, yl_ref, zu_ref, zl_ref, work, cy_own, cz_own, low, upt, from_up, from_low,
    prod_up, prod_low, send_sem, recv_sem
):
    rows = x_ref.shape[0]
    dom = lax.axis_index("dom")
    line = lax.axis_index("help")
    spot = lax.rem(dom, PLANE)
    exists = (
        (line < line_count - 1, line > 0),
        (spot < PLANE - 1, spot > 0),
        (dom + PLANE < dom_count, dom >= PLANE),
    )
    target = (
        ((dom, line + 1), (dom, line - 1)),
        ((dom + 1, line), (dom - 1, line)),
        ((dom + PLANE, line), (dom - PLANE, line)),
    )
    barrier = pltpu.get_barrier_semaphore()
    partners = jnp.int32(0)
    for d in range(3):
        for s in range(2):
            partners = partners + exists[d][s].astype(jnp.int32)

            @pl.when(exists[d][s])
            def _(d=d, s=s):
                pl.semaphore_signal(
                    barrier, inc=1, device_id=target[d][s], device_id_type=pl.DeviceIdType.MESH
                )

    pl.semaphore_wait(barrier, partners)
    messages = []

    def send(d, s, src, dst):
        m = len(messages)
        copy = pltpu.make_async_remote_copy(
            src_ref=src,
            dst_ref=dst,
            send_sem=send_sem.at[m],
            recv_sem=recv_sem.at[m],
            device_id=target[d][s],
            device_id_type=pl.DeviceIdType.MESH,
        )
        messages.append((d, s, copy))

        @pl.when(exists[d][s])
        def _():
            copy.start()

        return m

    def received(ids):
        for m in ids:
            d, s, copy = messages[m]

            @pl.when(exists[d][1 - s])
            def _(copy=copy):
                copy.wait_recv()

    def blank(d, s, ref):
        @pl.when(jnp.logical_not(exists[d][s]))
        def _():
            ref[...] = jnp.zeros_like(ref)

    blank(0, 1, edge_ref)
    blank(1, 1, cy_ref)
    blank(2, 1, cz_ref)
    blank(0, 1, dx_ref.at[0])
    blank(0, 0, dx_ref.at[rows + 1])
    blank(1, 0, yu_ref)
    blank(1, 1, yl_ref)
    blank(2, 0, zu_ref)
    blank(2, 1, zl_ref)
    for d in range(3):
        blank(d, 0, from_up.at[d])
        blank(d, 1, from_low.at[d])
        blank(d, 0, prod_up.at[d])
        blank(d, 1, prod_low.at[d])
    first = [send(d, 1, x_ref, from_up.at[d]) for d in range(3)]
    late = [send(0, 0, up_ref.at[rows - 1, 0], edge_ref.at[0])]
    cy_own[...] = up_ref[:, 1].astype(BF16)
    cz_own[...] = up_ref[:, 2].astype(BF16)
    vec = x_ref[...]
    at_row = lax.broadcasted_iota(jnp.int32, vec.shape, 0)
    for d in range(3):
        total = jnp.zeros_like(vec)
        for r in range(rows):
            total = jnp.where(at_row == r, mm(vec, up_ref[r, d], 1, 0), total)
        upt[d] = total
    for d in range(3):
        first.append(send(d, 0, upt.at[d], from_low.at[d]))
    late.append(send(1, 0, cy_own, cy_ref))
    late.append(send(2, 0, cz_own, cz_ref))
    work[...] = diag_ref[...]

    def above(own, edge):
        return jnp.where(at_row == rows - 1, edge[:1], pltpu.roll(own, rows - 1, 0))

    def below(own, edge):
        return jnp.where(at_row == 0, edge[rows - 1 : rows], pltpu.roll(own, 1, 0))

    def between(j):
        if j == work.shape[1] // SUB - 1:
            received(first)
            total = below(upt[0], from_low[0]) + from_low[1] + from_low[2]
            ups = [above(vec, from_up[0]), from_up[1], from_up[2]]
            for r in range(rows):
                part = mm(vec, diag_ref[r], 1, 1)
                for d in range(3):
                    part = part + mm(ups[d], up_ref[r, d], 1, 1)
                total = total + jnp.where(at_row == r, part, 0.0)
            prod_ref[...] = total
        if j == work.shape[1] // SUB - 2:
            for d in range(3):
                late.append(send(d, 1, prod_ref, prod_up.at[d]))
                late.append(send(d, 0, prod_ref, prod_low.at[d]))

    ul_factors(work, between)
    half = rows // 2
    for h in range(2):
        for r in range(half * h, half * h + half):
            y = work[r]
            inv = mm(y, y, 0, 0)
            dx_ref[r + 1] = inv
            low[r] = inv.astype(BF16)
        part = pl.ds(half * h, half)
        late.append(send(2, 0, low.at[part], zl_ref.at[part]))
        late.append(send(2, 1, low.at[part], zu_ref.at[part]))
        late.append(send(1, 0, low.at[part], yl_ref.at[part]))
        late.append(send(1, 1, low.at[part], yu_ref.at[part]))
        if h:
            late.append(send(0, 0, dx_ref.at[rows], dx_ref.at[0]))
        else:
            late.append(send(0, 1, dx_ref.at[1], dx_ref.at[rows + 1]))
    received(late)
    total = prod_ref[...]
    near_ref[0] = above(total, prod_up[0])
    near_ref[1] = below(total, prod_low[0])
    near_ref[2] = prod_up[1]
    near_ref[3] = prod_low[1]
    near_ref[4] = prod_up[2]
    near_ref[5] = prod_low[2]
    for d, s, copy in messages:

        @pl.when(exists[d][s])
        def _(copy=copy):
            copy.wait_send()


def rows_kernel(
    pattern_ref, diag_ref, up_ref, edge_ref, dx_ref, cy_ref, cz_ref, yu_ref, yl_ref, zu_ref,
    zl_ref, prod_ref, near_ref, factor_ref, applied_ref, work, solved
):
    count = work.shape[0]

    def gather(r, carry):
        schur = diag_ref[r]

        def term(k, inv, coupling, plus, mul):
            w = pattern_ref[r, k].astype(F32) * mul(inv, coupling, 1, 1 if plus else 0)
            solved[r, k] = w
            return mul(coupling, w, 1 if plus else 0, 0)

        lower = jnp.where(r == 0, edge_ref[0], up_ref[jnp.maximum(r - 1, 0), 0])
        schur = schur - term(0, dx_ref[r + 2], up_ref[r, 0], True, mm3)
        schur = schur - term(1, dx_ref[r], lower, False, mm3)
        schur = schur - term(2, yu_ref[r], up_ref[r, 1], True, mm1)
        schur = schur - term(3, yl_ref[r], cy_ref[r], False, mm1)
        schur = schur - term(4, zu_ref[r], up_ref[r, 2], True, mm1)
        schur = schur - term(5, zl_ref[r], cz_ref[r], False, mm1)
        work[r] = schur
        return carry

    lax.fori_loop(0, count, gather, 0)
    ul_factors(work)

    def split(v):
        high = v.astype(BF16).astype(F32)
        rest = v - high
        mid = rest.astype(BF16).astype(F32)
        return jnp.concatenate([high, mid, rest - mid], 0)

    def finish(r, carry):
        y = work[r]
        low = y.astype(BF16)
        factor_ref[r, 0] = low
        total = mm1(split(prod_ref[...]), low, 1, 1)
        for k in range(6):
            block = (-(mm3 if k < 2 else mm1)(y, solved[r, k], 1, 1)).astype(BF16)
            factor_ref[r, 1 + k] = block
            total = total + mm1(split(near_ref[k]), block, 1, 1)
        total = total[:count] + total[count : 2 * count] + total[2 * count :]
        keep = lax.broadcasted_iota(jnp.int32, total.shape, 0) == r
        applied_ref[...] = jnp.where(keep, total, applied_ref[...])
        return carry

    applied_ref[...] = jnp.zeros_like(applied_ref)
    lax.fori_loop(0, count, finish, 0)


VM = pl.BlockSpec(memory_space=pltpu.VMEM)
SM = pl.BlockSpec(memory_space=pltpu.SMEM)


def local(diag_blocks, up_blocks, pattern, vector_in):
    rows, width = diag_blocks.shape[0], diag_blocks.shape[1]
    block = jax.ShapeDtypeStruct((rows, width, width), BF16)
    vec = pltpu.VMEM((3, rows, width), F32)
    stack = pltpu.VMEM((rows, width, width), BF16)
    prod, near, dx, edge, cy, cz, yu, yl, zu, zl = pl.pallas_call(
        functools.partial(exchange_kernel, lax.axis_size("help"), lax.axis_size("dom")),
        out_shape=(
            jax.ShapeDtypeStruct((rows, width), F32),
            jax.ShapeDtypeStruct((6, rows, width), F32),
            jax.ShapeDtypeStruct((rows + 2, width, width), F32),
            jax.ShapeDtypeStruct((1, width, width), F32),
        )
        + (block,) * 6,
        in_specs=[VM] * 3,
        out_specs=(VM,) * 10,
        scratch_shapes=[pltpu.VMEM((rows, width, width), F32)]
        + [stack] * 3
        + [vec] * 5
        + [pltpu.SemaphoreType.DMA((MESSAGES,)), pltpu.SemaphoreType.DMA((MESSAGES,))],
        name="exchange",
        compiler_params=pltpu.CompilerParams(
            collective_id=0, has_side_effects=True, vmem_limit_bytes=40 << 20
        ),
    )(diag_blocks, up_blocks, vector_in)
    factor, applied = pl.pallas_call(
        rows_kernel,
        out_shape=(
            jax.ShapeDtypeStruct((rows, 7, width, width), BF16),
            jax.ShapeDtypeStruct((rows, width), F32),
        ),
        in_specs=[SM] + [VM] * 12,
        out_specs=(VM, VM),
        scratch_shapes=[
            pltpu.VMEM((rows, width, width), F32),
            pltpu.VMEM((rows, 6, width, width), F32),
        ],
        name="rows",
        compiler_params=pltpu.CompilerParams(vmem_limit_bytes=40 << 20),
    )(pattern, diag_blocks, up_blocks, edge, dx, cy, cz, yu, yl, zu, zl, prod, near)
    return (factor, applied)


def solution(mesh):
    in_specs = (
        P(("dom", "help"), None, None),
        P(("dom", "help"), None, None, None),
        P(("dom", "help"), None),
        P(("dom", "help"), None),
    )
    out_specs = (P(("dom", "help"), None, None, None), P(("dom", "help"), None))
    return jax.shard_map(local, mesh=mesh, in_specs=in_specs, out_specs=out_specs, check_vma=False)
```

time: 153 us -> 64.6 us (0.42)
  the two profiles are of different devices: /device:TPU:10 before, /device:TPU:0 now
where the time goes in v2:
time: 64.6 us; the launch traced here: 64.4 us
  Pallas kernels  60.6 us (94%)
  local copies, waits for them, and re-layouts  3.13 us (5%)
  between operations  0.66 us (1%)
    pallas_call x1, Pallas kernels, local(): pl.pallas_call(rows_kernel, out_shape=(jax.ShapeDtypeStruct((rows, 7, wid...  31.9 us
    pallas_call x1, Pallas kernels, local(): pl.pallas_call(functools.partial(exchange_kernel, lax.axis_size('help'),...  28.7 us
    unnamed x8, local copies, waits for them, and re-layouts  3.13 us

profile of v2, /device:TPU:0, one launch (start us, length us, event | category | flops | bytes accessed | tf_op | source)
XLA Modules:
  0.0 64.4 jit_solution(17570582196231972993)
XLA Ops:
  0.6 0.0 copy-start
  0.6 1.4 %copy-done = f32[8,3,128,128]{3,2,1,0:T(8,128)S(1)} copy-done((f32[8,3,128,128]{3,2,1,0:T(8,128)S(1)}, f32[8,3,128,128]{3,2,1,0:T(8,128)}, u32[]{:S(2)}) %copy-start) | copy-done | bytes 1572888
  2.0 0.0 copy-start.1
  2.0 1.0 %copy-done.1 = f32[8,128,128]{2,1,0:T(8,128)S(1)} copy-done((f32[8,128,128]{2,1,0:T(8,128)S(1)}, f32[8,128,128]{2,1,0:T(8,128)}, u32[]{:S(2)}) %copy-start.1) | copy-done | bytes 524312
  3.1 0.0 copy-start.2
  3.1 0.7 %copy-done.2 = f32[8,128]{1,0:T(8,128)S(1)} copy-done((f32[8,128]{1,0:T(8,128)S(1)}, f32[8,128]{1,0:T(8,128)}, u32[]{:S(2)}) %copy-start.2) | copy-done | bytes 4120
  3.8 0.0 copy-start.3
  3.8 28.7 %exchange.1 = (f32[8,128]{1,0:T(8,128)S(1)}, f32[6,8,128]{2,1,0:T(8,128)S(1)}, f32[10,128,128]{2,1,0:T(8,128)S(1)}, f32[1,128,128]{2,1,0:T(8,128)S(1)}, bf16[8,1...) custom-call(f32[8,128,128]{2,1,0:T(8,128)S(1)} %copy-done.1, ...), custom_call_target="tpu_custom_call" | custom-call | tf_op jit(solution)/shard_map/exchange/pallas_call | solution.py:309
  32.5 0.0 copy-done.3
  32.5 31.9 %rows.1 = (bf16[8,7,128,128]{3,2,1,0:T(8,128)(2,1)}, f32[8,128]{1,0:T(8,128)}) custom-call(s32[8,6]{1,0:T(8,128)S(1)} %copy-done.3, f32[8,128,128]{2,1,0:T(8,128)S(1)} %copy-done.1, f32[8,3,128,128]{3,2,1,0:T(8,128)S(1)} %copy-done, f32[1,128,128]{2,1,0:T(8,128)S(1)} %get-tuple-element.12.edge_ref, f32[10,128,128]{2,1,0:T(8,128)S(1)} %get-tuple-element.13.dx_ref, ...), custom_call_target="tpu_custom_call" | custom-call | tf_op jit(solution)/shard_map/rows/pallas_call | solution.py:329
Async XLA Ops:
  0.6 1.4 %copy-start = (f32[8,3,128,128]{3,2,1,0:T(8,128)S(1)}, f32[8,3,128,128]{3,2,1,0:T(8,128)}, u32[]{:S(2)}) copy-start(f32[8,3,128,128]{3,2,1,0:T(8,128)} %up_ref.3) | copy-start | bytes 4718596
  2.0 1.0 %copy-start.1 = (f32[8,128,128]{2,1,0:T(8,128)S(1)}, f32[8,128,128]{2,1,0:T(8,128)}, u32[]{:S(2)}) copy-start(f32[8,128,128]{2,1,0:T(8,128)} %diag_ref.3) | copy-start | bytes 1572868
  3.1 0.7 %copy-start.2 = (f32[8,128]{1,0:T(8,128)S(1)}, f32[8,128]{1,0:T(8,128)}, u32[]{:S(2)}) copy-start(f32[8,128]{1,0:T(8,128)} %x_ref.1) | copy-start | bytes 12292
  3.8 28.7 %copy-start.3 = (s32[8,6]{1,0:T(8,128)S(1)}, s32[8,6]{1,0:T(8,128)}, u32[]{:S(2)}) copy-start(s32[8,6]{1,0:T(8,128)} %pattern_ref.1) | copy-start | bytes 580

commit v3 on v2

--- a/solution.py
+++ b/solution.py
@@ -37,24 +37,50 @@
     return mm1(ah, bh, ca, cb) + (mm1(ah, bl, ca, cb) + mm1(al, bh, ca, cb))
 
 
-def small_factors(tiles):
+def split(v):
+    high = v.astype(BF16).astype(F32)
+    rest = v - high
+    mid = rest.astype(BF16).astype(F32)
+    return jnp.concatenate([high, mid, rest - mid], 0).astype(BF16)
+
+
+def mv(parts, matrix, cb):
+    high, low = halves(matrix)
+    total = mm1(parts, high, 1, cb) + mm1(parts, low, 1, cb)
+    n = total.shape[0] // 3
+    return total[:n] + (total[n : 2 * n] + total[2 * n :])
+
+
+def small_factors(groups):
     lane = lax.broadcasted_iota(jnp.int32, (8, 128), 1)
     sub = lax.broadcasted_iota(jnp.int32, (8, 128), 0)
     within = lane % SUB
     base = lane - within
-    for j in range(SUB - 1, -1, -1):
-        top, at = j // 8, j % 8
-        here = within == j
-        cols = [jnp.take_along_axis(tiles[t], base + j, axis=1) for t in range(top + 1)]
-        scale = lax.rsqrt(cols[top][at : at + 1, :])
-        row = jnp.where(here[:1], 1.0, tiles[top][at : at + 1, :]) * scale
-        final = jnp.where(within[:1] >= j, row, 0.0)
-        for t in range(top + 1):
-            new = jnp.where(here, 0.0, tiles[t]) - (cols[t] * scale) * row
-            if t == top:
-                new = jnp.where(sub < at, new, jnp.where(sub == at, final, tiles[t]))
-            tiles[t] = new
-    return tiles
+    for top in range(SUB // 8 - 1, -1, -1):
+        ahead = [
+            [
+                [jnp.take_along_axis(tiles[t], base + 8 * top + i, axis=1) for t in range(top + 1)]
+                for i in range(8)
+            ]
+            for tiles in groups
+        ]
+        for at in range(7, -1, -1):
+            j = 8 * top + at
+            here = within == j
+            for tiles, cols in zip(groups, ahead):
+                scale = lax.rsqrt(cols[at][top][at : at + 1, :])
+                scaled = [cols[at][t] * scale for t in range(top + 1)]
+                for i in range(at - 1, -1, -1):
+                    weight = cols[i][top][at : at + 1, :] * scale
+                    cols[i] = [cols[i][t] - scaled[t] * weight for t in range(top + 1)]
+                row = jnp.where(here[:1], 1.0, tiles[top][at : at + 1, :]) * scale
+                final = jnp.where(within[:1] >= j, row, 0.0)
+                for t in range(top + 1):
+                    new = jnp.where(here, 0.0, tiles[t]) - scaled[t] * row
+                    if t == top:
+                        new = jnp.where(sub < at, new, jnp.where(sub == at, final, tiles[t]))
+                    tiles[t] = new
+    return groups
 
 
 def ul_factors(work, between=None):
@@ -78,18 +104,19 @@
                 panel.append(jnp.where(owner == j, (lane - lo == sub).astype(F32), rows))
             packed.append([block[8 * t : 8 * t + 8] for t in range(SUB // 8)])
             panels.append(jnp.concatenate(panel, 0))
+        small_factors(packed)
         for g in range(count // pack):
-            small = jnp.concatenate(small_factors(packed[g]), 0)
+            small = jnp.concatenate(packed[g], 0)
             spread = jnp.concatenate(
                 [jnp.where(owner == b, small, 0.0) for b in range(pack)], 0
             )
-            scaled = mm(spread, panels[g], 1, 0)
+            scaled = mm3(spread, panels[g], 1, 0)
             for b in range(pack):
                 at = g * pack + b
                 v = scaled[SUB * b : SUB * b + SUB]
                 work[at, lo : lo + SUB, :] = jnp.where(lane >= lo, v, 0.0)
                 if lo:
-                    change = mm(v, v, 0, 0)
+                    change = mm3(v, v, 0, 0)
                     full = lax.broadcasted_iota(jnp.int32, (lo, width), 1) // SUB
                     work[at, :lo, :] = jnp.where(full == j, 0.0, work[at, :lo, :]) - change[:lo]
         if between:
@@ -180,11 +207,12 @@
     cy_own[...] = up_ref[:, 1].astype(BF16)
     cz_own[...] = up_ref[:, 2].astype(BF16)
     vec = x_ref[...]
+    parts = split(vec)
     at_row = lax.broadcasted_iota(jnp.int32, vec.shape, 0)
     for d in range(3):
         total = jnp.zeros_like(vec)
         for r in range(rows):
-            total = jnp.where(at_row == r, mm(vec, up_ref[r, d], 1, 0), total)
+            total = jnp.where(at_row == r, mv(parts, up_ref[r, d], 0), total)
         upt[d] = total
     for d in range(3):
         first.append(send(d, 0, upt.at[d], from_low.at[d]))
@@ -202,11 +230,11 @@
         if j == work.shape[1] // SUB - 1:
             received(first)
             total = below(upt[0], from_low[0]) + from_low[1] + from_low[2]
-            ups = [above(vec, from_up[0]), from_up[1], from_up[2]]
+            ups = [split(v) for v in (above(vec, from_up[0]), from_up[1], from_up[2])]
             for r in range(rows):
-                part = mm(vec, diag_ref[r], 1, 1)
+                part = mv(parts, diag_ref[r], 1)
                 for d in range(3):
-                    part = part + mm(ups[d], up_ref[r, d], 1, 1)
+                    part = part + mv(ups[d], up_ref[r, d], 1)
                 total = total + jnp.where(at_row == r, part, 0.0)
             prod_ref[...] = total
         if j == work.shape[1] // SUB - 2:
@@ -219,7 +247,7 @@
     for h in range(2):
         for r in range(half * h, half * h + half):
             y = work[r]
-            inv = mm(y, y, 0, 0)
+            inv = mm3(y, y, 0, 0)
             dx_ref[r + 1] = inv
             low[r] = inv.astype(BF16)
         part = pl.ds(half * h, half)
@@ -270,31 +298,28 @@
         work[r] = schur
         return carry
 
-    lax.fori_loop(0, count, gather, 0)
+    lax.fori_loop(0, count, gather, 0, unroll=2)
     ul_factors(work)
 
-    def split(v):
-        high = v.astype(BF16).astype(F32)
-        rest = v - high
-        mid = rest.astype(BF16).astype(F32)
-        return jnp.concatenate([high, mid, rest - mid], 0)
+    own = split(prod_ref[...])
+    around = [split(near_ref[k]) for k in range(6)]
 
     def finish(r, carry):
         y = work[r]
         low = y.astype(BF16)
         factor_ref[r, 0] = low
-        total = mm1(split(prod_ref[...]), low, 1, 1)
+        total = mm1(own, low, 1, 1)
         for k in range(6):
             block = (-(mm3 if k < 2 else mm1)(y, solved[r, k], 1, 1)).astype(BF16)
             factor_ref[r, 1 + k] = block
-            total = total + mm1(split(near_ref[k]), block, 1, 1)
+            total = total + mm1(around[k], block, 1, 1)
         total = total[:count] + total[count : 2 * count] + total[2 * count :]
         keep = lax.broadcasted_iota(jnp.int32, total.shape, 0) == r
         applied_ref[...] = jnp.where(keep, total, applied_ref[...])
         return carry
 
     applied_ref[...] = jnp.zeros_like(applied_ref)
-    lax.fori_loop(0, count, finish, 0)
+    lax.fori_loop(0, count, finish, 0, unroll=2)
 
 
 VM = pl.BlockSpec(memory_space=pltpu.VMEM)

time: 64.6 us -> 44.8 us (0.69)
  Pallas kernels: 60.6 us -> 40.7 us
    pallas_call x1, Pallas kernels: 31.9 us -> 20.9 us  [local(): pl.pallas_call(rows_kernel, out_shape=(jax.ShapeDtypeStruct((rows, 7, wid...]
    pallas_call x1, Pallas kernels: 28.7 us -> 19.8 us  [local(): pl.pallas_call(functools.partial(exchange_kernel, lax.axis_size('help'),...]
where the time goes in v3:
time: 44.8 us; the launch traced here: 44.5 us
  Pallas kernels  40.7 us (91%)
  local copies, waits for them, and re-layouts  3.13 us (7%)
  between operations  0.66 us (1%)
    pallas_call x1, Pallas kernels, local(): pl.pallas_call(rows_kernel, out_shape=(jax.ShapeDtypeStruct((rows, 7, wid...  20.9 us
    pallas_call x1, Pallas kernels, local(): pl.pallas_call(functools.partial(exchange_kernel, lax.axis_size('help'),...  19.8 us
    unnamed x8, local copies, waits for them, and re-layouts  3.13 us

profile of v3, /device:TPU:0, one launch (start us, length us, event | category | flops | bytes accessed | tf_op | source)
XLA Modules:
  0.0 44.5 jit_solution(9043663746989345988)
XLA Ops:
  0.6 0.0 copy-start
  0.6 1.4 %copy-done = f32[8,3,128,128]{3,2,1,0:T(8,128)S(1)} copy-done((f32[8,3,128,128]{3,2,1,0:T(8,128)S(1)}, f32[8,3,128,128]{3,2,1,0:T(8,128)}, u32[]{:S(2)}) %copy-start) | copy-done | bytes 1572888
  2.0 0.0 copy-start.1
  2.0 1.0 %copy-done.1 = f32[8,128,128]{2,1,0:T(8,128)S(1)} copy-done((f32[8,128,128]{2,1,0:T(8,128)S(1)}, f32[8,128,128]{2,1,0:T(8,128)}, u32[]{:S(2)}) %copy-start.1) | copy-done | bytes 524312
  3.1 0.0 copy-start.2
  3.1 0.7 %copy-done.2 = f32[8,128]{1,0:T(8,128)S(1)} copy-done((f32[8,128]{1,0:T(8,128)S(1)}, f32[8,128]{1,0:T(8,128)}, u32[]{:S(2)}) %copy-start.2) | copy-done | bytes 4120
  3.8 0.0 copy-start.3
  3.8 19.8 %exchange.1 = (f32[8,128]{1,0:T(8,128)S(1)}, f32[6,8,128]{2,1,0:T(8,128)S(1)}, f32[10,128,128]{2,1,0:T(8,128)S(1)}, f32[1,128,128]{2,1,0:T(8,128)S(1)}, bf16[8,1...) custom-call(f32[8,128,128]{2,1,0:T(8,128)S(1)} %copy-done.1, ...), custom_call_target="tpu_custom_call" | custom-call | tf_op jit(solution)/shard_map/exchange/pallas_call | solution.py:334
  23.6 0.0 copy-done.3
  23.6 20.9 %rows.1 = (bf16[8,7,128,128]{3,2,1,0:T(8,128)(2,1)}, f32[8,128]{1,0:T(8,128)}) custom-call(s32[8,6]{1,0:T(8,128)S(1)} %copy-done.3, f32[8,128,128]{2,1,0:T(8,128)S(1)} %copy-done.1, f32[8,3,128,128]{3,2,1,0:T(8,128)S(1)} %copy-done, f32[1,128,128]{2,1,0:T(8,128)S(1)} %get-tuple-element.12.edge_ref, f32[10,128,128]{2,1,0:T(8,128)S(1)} %get-tuple-element.13.dx_ref, ...), custom_call_target="tpu_custom_call" | custom-call | tf_op jit(solution)/shard_map/rows/pallas_call | solution.py:354
Async XLA Ops:
  0.6 1.4 %copy-start = (f32[8,3,128,128]{3,2,1,0:T(8,128)S(1)}, f32[8,3,128,128]{3,2,1,0:T(8,128)}, u32[]{:S(2)}) copy-start(f32[8,3,128,128]{3,2,1,0:T(8,128)} %up_ref.3) | copy-start | bytes 4718596
  2.0 1.0 %copy-start.1 = (f32[8,128,128]{2,1,0:T(8,128)S(1)}, f32[8,128,128]{2,1,0:T(8,128)}, u32[]{:S(2)}) copy-start(f32[8,128,128]{2,1,0:T(8,128)} %diag_ref.3) | copy-start | bytes 1572868
  3.1 0.7 %copy-start.2 = (f32[8,128]{1,0:T(8,128)S(1)}, f32[8,128]{1,0:T(8,128)}, u32[]{:S(2)}) copy-start(f32[8,128]{1,0:T(8,128)} %x_ref.1) | copy-start | bytes 12292
  3.8 19.8 %copy-start.3 = (s32[8,6]{1,0:T(8,128)S(1)}, s32[8,6]{1,0:T(8,128)}, u32[]{:S(2)}) copy-start(s32[8,6]{1,0:T(8,128)} %pattern_ref.1) | copy-start | bytes 580

commit v4 on v3

--- a/solution.py
+++ b/solution.py
@@ -9,7 +9,8 @@
 
 PLANE = 4
 SUB = 32
-MESSAGES = 25
+CHUNKS = 4
+MESSAGES = 17 + 4 * CHUNKS
 HIGH = lax.Precision.HIGHEST
 F32 = jnp.float32
 BF16 = jnp.bfloat16
@@ -243,8 +244,8 @@
                 late.append(send(d, 0, prod_ref, prod_low.at[d]))
 
     ul_factors(work, between)
-    half = rows // 2
-    for h in range(2):
+    half = rows // CHUNKS
+    for h in range(CHUNKS):
         for r in range(half * h, half * h + half):
             y = work[r]
             inv = mm3(y, y, 0, 0)
@@ -255,9 +256,9 @@
         late.append(send(2, 1, low.at[part], zu_ref.at[part]))
         late.append(send(1, 0, low.at[part], yl_ref.at[part]))
         late.append(send(1, 1, low.at[part], yu_ref.at[part]))
-        if h:
+        if h == CHUNKS - 1:
             late.append(send(0, 0, dx_ref.at[rows], dx_ref.at[0]))
-        else:
+        if h == 0:
             late.append(send(0, 1, dx_ref.at[1], dx_ref.at[rows + 1]))
     received(late)
     total = prod_ref[...]
@@ -298,7 +299,7 @@
         work[r] = schur
         return carry
 
-    lax.fori_loop(0, count, gather, 0, unroll=2)
+    lax.fori_loop(0, count, gather, 0, unroll=4)
     ul_factors(work)
 
     own = split(prod_ref[...])
@@ -319,7 +320,7 @@
         return carry
 
     applied_ref[...] = jnp.zeros_like(applied_ref)
-    lax.fori_loop(0, count, finish, 0, unroll=2)
+    lax.fori_loop(0, count, finish, 0, unroll=4)
 
 
 VM = pl.BlockSpec(memory_space=pltpu.VMEM)

time: 44.8 us -> 43.8 us (0.978)
  Pallas kernels: 40.7 us -> 39.8 us
    pallas_call x1, Pallas kernels: 20.9 us -> 19.9 us  [local(): pl.pallas_call(rows_kernel, out_shape=(jax.ShapeDtypeStruct((rows, 7, wid...]
where the time goes in v4:
time: 43.8 us; the launch traced here: 43.6 us
  Pallas kernels  39.8 us (91%)
  local copies, waits for them, and re-layouts  3.13 us (7%)
  between operations  0.66 us (2%)
    pallas_call x1, Pallas kernels, local(): pl.pallas_call(rows_kernel, out_shape=(jax.ShapeDtypeStruct((rows, 7, wid...  19.9 us
    pallas_call x1, Pallas kernels, local(): pl.pallas_call(functools.partial(exchange_kernel, lax.axis_size('help'),...  19.9 us
    unnamed x8, local copies, waits for them, and re-layouts  3.13 us

profile of v4, /device:TPU:0, one launch (start us, length us, event | category | flops | bytes accessed | tf_op | source)
XLA Modules:
  0.0 43.6 jit_solution(7901944448064240564)
XLA Ops:
  0.6 0.0 copy-start
  0.6 1.4 %copy-done = f32[8,3,128,128]{3,2,1,0:T(8,128)S(1)} copy-done((f32[8,3,128,128]{3,2,1,0:T(8,128)S(1)}, f32[8,3,128,128]{3,2,1,0:T(8,128)}, u32[]{:S(2)}) %copy-start) | copy-done | bytes 1572888
  2.0 0.0 copy-start.1
  2.0 1.0 %copy-done.1 = f32[8,128,128]{2,1,0:T(8,128)S(1)} copy-done((f32[8,128,128]{2,1,0:T(8,128)S(1)}, f32[8,128,128]{2,1,0:T(8,128)}, u32[]{:S(2)}) %copy-start.1) | copy-done | bytes 524312
  3.1 0.0 copy-start.2
  3.1 0.7 %copy-done.2 = f32[8,128]{1,0:T(8,128)S(1)} copy-done((f32[8,128]{1,0:T(8,128)S(1)}, f32[8,128]{1,0:T(8,128)}, u32[]{:S(2)}) %copy-start.2) | copy-done | bytes 4120
  3.8 0.0 copy-start.3
  3.8 19.9 %exchange.1 = (f32[8,128]{1,0:T(8,128)S(1)}, f32[6,8,128]{2,1,0:T(8,128)S(1)}, f32[10,128,128]{2,1,0:T(8,128)S(1)}, f32[1,128,128]{2,1,0:T(8,128)S(1)}, bf16[8,1...) custom-call(f32[8,128,128]{2,1,0:T(8,128)S(1)} %copy-done.1, ...), custom_call_target="tpu_custom_call" | custom-call | tf_op jit(solution)/shard_map/exchange/pallas_call | solution.py:335
  23.7 0.0 copy-done.3
  23.7 19.9 %rows.1 = (bf16[8,7,128,128]{3,2,1,0:T(8,128)(2,1)}, f32[8,128]{1,0:T(8,128)}) custom-call(s32[8,6]{1,0:T(8,128)S(1)} %copy-done.3, f32[8,128,128]{2,1,0:T(8,128)S(1)} %copy-done.1, f32[8,3,128,128]{3,2,1,0:T(8,128)S(1)} %copy-done, f32[1,128,128]{2,1,0:T(8,128)S(1)} %get-tuple-element.12.edge_ref, f32[10,128,128]{2,1,0:T(8,128)S(1)} %get-tuple-element.13.dx_ref, ...), custom_call_target="tpu_custom_call" | custom-call | tf_op jit(solution)/shard_map/rows/pallas_call | solution.py:355
Async XLA Ops:
  0.6 1.4 %copy-start = (f32[8,3,128,128]{3,2,1,0:T(8,128)S(1)}, f32[8,3,128,128]{3,2,1,0:T(8,128)}, u32[]{:S(2)}) copy-start(f32[8,3,128,128]{3,2,1,0:T(8,128)} %up_ref.3) | copy-start | bytes 4718596
  2.0 1.0 %copy-start.1 = (f32[8,128,128]{2,1,0:T(8,128)S(1)}, f32[8,128,128]{2,1,0:T(8,128)}, u32[]{:S(2)}) copy-start(f32[8,128,128]{2,1,0:T(8,128)} %diag_ref.3) | copy-start | bytes 1572868
  3.1 0.7 %copy-start.2 = (f32[8,128]{1,0:T(8,128)S(1)}, f32[8,128]{1,0:T(8,128)}, u32[]{:S(2)}) copy-start(f32[8,128]{1,0:T(8,128)} %x_ref.1) | copy-start | bytes 12292
  3.8 19.9 %copy-start.3 = (s32[8,6]{1,0:T(8,128)S(1)}, s32[8,6]{1,0:T(8,128)}, u32[]{:S(2)}) copy-start(s32[8,6]{1,0:T(8,128)} %pattern_ref.1) | copy-start | bytes 580
